TPU v7x, 256 devices: a whole 4x4x8 slice. The times are simulated.
256 devices in a mesh: segment: 8 (over x, core), graph: 32 (over y, z).
Axes of the slice: x: 4, y: 4, z: 8, core: 2. Of those that a mesh axis runs over, the one named last changes fastest.
Arguments:
- state: float32 [8, 16384, 1024], P('segment', 'graph'), may hold values from -6 to 6
- initial: float32 [8, 16384, 1024], P('segment', 'graph'), may hold values from -6 to 6
- fresh: float32 [16384, 1024], P('graph'), may hold values from -6 to 6
- weights: float32 [8, 1024, 1024], P('segment'), may hold values from -0.1875 to 0.1875
- wants: int32 [32, 4, 1], P('graph'), may hold values from 0 to 3
- adj_slot: int32 [128, 4], P('graph'), may hold values from 0 to 7, as said below
- adj_count: int32 [128], P('graph'), may hold values from 2 to 4, as said below
- adj_vals: float32 [128, 4, 128, 128], P('graph'), may hold values from -0.25 to 0.25
Outputs:
- handed: float32 [8, 16384, 1024], P('segment', 'graph')
- advanced: float32 [8, 16384, 1024], P('segment', 'graph')
Inputs may be any that keep to these rules, and one draw needn't show every extreme that they name: `adj_slot`: every entry of a destination block's row at k < 2 names a slot past the partition's own blocks, and every such slot of a partition is named at some k < 2 of one of its blocks. `adj_count`: each partition has a block with exactly 4 nonzero blocks.
All inputs are finite; a program needn't handle non-finite values.
Results may differ from a plain program's by a relative error of at most 0.0001.
Values sent between devices are 32-bit elements; how exact they have to be, the bound alone decides.
A program may use at most 128 MiB of HBM per device.

v0:
```python
import jax
import jax.numpy as jnp
from jax import lax
from jax.sharding import PartitionSpec as P

D = 1024
BLK = 128
KMAX = 4
REACH = 2


def from_behind(value, axis, by):
    peers = lax.axis_size(axis)
    pairs = [(i, i + by) for i in range(peers) if 0 <= i + by < peers]
    return lax.ppermute(value, axis, pairs)


def offset_list():
    found = []
    for radius in range(1, REACH + 1):
        found.append(radius)
        found.append(-radius)
    return found


def local_layer(feats, first_feats, weight, layer_index, received, adj_slot, adj_count, adj_vals):
    nblocks = feats.shape[0] // BLK
    row_blocks = feats.reshape(nblocks, BLK, D)
    sources = jnp.concatenate([row_blocks, received], axis=0)
    selected = sources[adj_slot]
    live = (jnp.arange(KMAX, dtype=jnp.int32)[None, :] < adj_count[:, None]).astype(jnp.float32)
    values = adj_vals * live[:, :, None, None]
    agg = jnp.einsum("bkij,bkjd->bid", values, selected, precision=lax.Precision.HIGHEST).reshape(
        feats.shape[0], D
    )
    mixed = 0.9 * agg + 0.1 * first_feats
    beta = jnp.log(0.5 / (layer_index + 1.0) + 1.0)
    product = jnp.dot(
        mixed, weight, precision=lax.Precision.HIGHEST, preferred_element_type=jnp.float32
    )
    return jax.nn.relu((1.0 - beta) * mixed + beta * product)


def shards(state, initial, fresh, weights, wants, adj_slot, adj_count, adj_vals):
    section = lax.axis_index("segment")
    layer_index = section.astype(jnp.float32)
    weight = weights[0]
    offsets = offset_list()
    asked = [
        from_behind(wants[0, position], "graph", -shift_by)
        for position, shift_by in enumerate(offsets)
    ]

    def fetch(feats):
        row_blocks = feats.reshape(feats.shape[0] // BLK, BLK, D)
        pieces = [
            from_behind(row_blocks[asked[position]], "graph", shift_by)
            for position, shift_by in enumerate(offsets)
        ]
        return jnp.concatenate(pieces, axis=0)

    feats = state[0]
    first_feats = initial[0]
    first_out = local_layer(
        feats, first_feats, weight, layer_index, fetch(feats), adj_slot, adj_count, adj_vals
    )
    came_feats, came_first = from_behind((first_out, first_feats), "segment", 1)
    is_first = section == 0
    next_feats = jnp.where(is_first, fresh, came_feats)
    next_first = jnp.where(is_first, fresh, came_first)
    second_out = local_layer(
        next_feats,
        next_first,
        weight,
        layer_index,
        fetch(next_feats),
        adj_slot,
        adj_count,
        adj_vals,
    )
    return (first_out[None], second_out[None])


def solution(mesh):
    return jax.shard_map(
        shards,
        mesh=mesh,
        in_specs=(
            P("segment", "graph", None),
            P("segment", "graph", None),
            P("graph", None),
            P("segment", None, None),
            P("graph", None, None),
            P("graph", None),
            P("graph"),
            P("graph", None, None, None),
        ),
        out_specs=(P("segment", "graph", None), P("segment", "graph", None)),
        check_vma=False,
    )
```

profile of v0, /device:TPU:82, one launch (start us, length us, event | category | flops | bytes accessed | tf_op | source)
XLA Modules:
  0.0 194.1 jit_solution(6676270653838565251)
XLA Ops:
  0.6 1.5 fusion.16
  2.1 2.0 %collective-permute-start = (s32[1]{0:T(128)}, s32[1]{0:T(128)}, u32[]{:S(2)}, u32[]{:S(2)}) collective-permute-start(s32[1]{0:T(128)} %bitcast.1), channel_id=1, source_target_pairs={{1,0},{2,1},{3,2},{4,3},{5,4},{6,5},{7,6},{8,7},{9,8},{10,9},{11,1... | collective-permute-start | bytes 20 | tf_op jit(solution)/shard_map/ppermute | solution.py:15
  4.1 3.8 %collective-permute-start.2 = (s32[1]{0:T(128)}, s32[1]{0:T(128)}, u32[]{:S(2)}, u32[]{:S(2)}) collective-permute-start(s32[1]{0:T(128)} %bitcast.3), channel_id=1, source_target_pairs={{0,1},{1,2},{2,3},{3,4},{4,5},{5,6},{6,7},{7,8},{8,9},{9,10},{10,1... | collective-permute-start | bytes 20 | tf_op jit(solution)/shard_map/ppermute | solution.py:15
  7.9 5.3 %collective-permute-start.4 = (s32[1]{0:T(128)}, s32[1]{0:T(128)}, u32[]{:S(2)}, u32[]{:S(2)}) collective-permute-start(s32[1]{0:T(128)} %bitcast.5), channel_id=1, source_target_pairs={{2,0},{3,1},{4,2},{5,3},{6,4},{7,5},{8,6},{9,7},{10,8},{11,9},{12,... | collective-permute-start | bytes 20 | tf_op jit(solution)/shard_map/ppermute | solution.py:15
  13.3 3.2 %collective-permute-start.6 = (s32[1]{0:T(128)}, s32[1]{0:T(128)}, u32[]{:S(2)}, u32[]{:S(2)}) collective-permute-start(s32[1]{0:T(128)} %bitcast.7), channel_id=1, source_target_pairs={{0,2},{1,3},{2,4},{3,5},{4,6},{5,7},{6,8},{7,9},{8,10},{9,11},{10,... | collective-permute-start | bytes 20 | tf_op jit(solution)/shard_map/ppermute | solution.py:15
  16.4 1.8 broadcast_multiply_fusion
  26.0 1.2 constant_dynamic-slice_fusion.4
  27.2 4.7 %collective-permute-start.1 = (f32[1,128,1024]{2,1,0:T(8,128)}, f32[1,128,1024]{2,1,0:T(8,128)S(1)}, u32[]{:S(2)}, u32[]{:S(2)}) collective-permute-start(f32[1,128,1024]{2,1,0:T(8,128)} %get-tuple-element.97), channel_id=1, source_target_pairs={{0,1},{1,2},{2,3},{3,4},{4,5},{5,6},{6,7},{7,8},{8,9},{9,10},{10,1... | collective-permute-start | bytes 1572872 | tf_op jit(solution)/shard_map/ppermute | solution.py:15
  31.9 0.1 reshape.215
  32.1 3.2 %collective-permute-start.3 = (f32[1,128,1024]{2,1,0:T(8,128)}, f32[1,128,1024]{2,1,0:T(8,128)S(1)}, u32[]{:S(2)}, u32[]{:S(2)}) collective-permute-start(f32[1,128,1024]{2,1,0:T(8,128)} %get-tuple-element.96), channel_id=1, source_target_pairs={{1,0},{2,1},{3,2},{4,3},{5,4},{6,5},{7,6},{8,7},{9,8},{10,9},{11,1... | collective-permute-start | bytes 1572872 | tf_op jit(solution)/shard_map/ppermute | solution.py:15
  35.3 0.1 fusion.15
  35.4 3.9 %collective-permute-start.5 = (f32[1,128,1024]{2,1,0:T(8,128)}, f32[1,128,1024]{2,1,0:T(8,128)S(1)}, u32[]{:S(2)}, u32[]{:S(2)}) collective-permute-start(f32[1,128,1024]{2,1,0:T(8,128)} %get-tuple-element.95), channel_id=1, source_target_pairs={{0,2},{1,3},{2,4},{3,5},{4,6},{5,7},{6,8},{7,9},{8,10},{9,11},{10,... | collective-permute-start | bytes 1572872 | tf_op jit(solution)/shard_map/ppermute | solution.py:15
  39.4 3.8 %collective-permute-start.7 = (f32[1,128,1024]{2,1,0:T(8,128)S(1)}, f32[1,128,1024]{2,1,0:T(8,128)S(1)}, u32[]{:S(2)}, u32[]{:S(2)}) collective-permute-start(f32[1,128,1024]{2,1,0:T(8,128)S(1)} %get-tuple-element.94), channel_id=1, source_target_pairs={{2,0},{3,1},{4,2},{5,3},{6,4},{7,5},{8,6},{9,7},{10,8},{11,9},{12,... | collective-permute-start | bytes 1572872 | tf_op jit(solution)/shard_map/ppermute | solution.py:15
  43.2 3.2 %constant_dynamic-update-slice_fusion.4 = f32[8,128,1024]{2,1,0:T(8,128)} fusion(f32[4,128,1024]{2,1,0:T(8,128)} %bitcast.54), kind=kLoop, calls=%fused_computation.24 | loop fusion | bytes 4194304
  46.4 3.2 %collective-permute-done.1 = f32[1,128,1024]{2,1,0:T(8,128)S(1)} collective-permute-done((f32[1,128,1024]{2,1,0:T(8,128)}, f32[1,128,1024]{2,1,0:T(8,128)S(1)}, u32[]{:S(2)}, u32[]{:S(2)}) %collective-permute-start.1) | collective-permute-done | bytes 524320 | tf_op jit(solution)/shard_map/ppermute | solution.py:15
  49.7 0.8 constant_dynamic-update-slice_fusion.3
  50.5 0.2 collective-permute-done.3
  50.7 0.8 constant_dynamic-update-slice_fusion.2
  51.6 14.1 %collective-permute-done.5 = f32[1,128,1024]{2,1,0:T(8,128)S(1)} collective-permute-done((f32[1,128,1024]{2,1,0:T(8,128)}, f32[1,128,1024]{2,1,0:T(8,128)S(1)}, u32[]{:S(2)}, u32[]{:S(2)}) %collective-permute-start.5) | collective-permute-done | bytes 524320 | tf_op jit(solution)/shard_map/ppermute | solution.py:15
  65.7 0.8 constant_dynamic-update-slice_fusion.1
  66.5 3.7 %collective-permute-done.7 = f32[1,128,1024]{2,1,0:T(8,128)S(1)} collective-permute-done((f32[1,128,1024]{2,1,0:T(8,128)S(1)}, f32[1,128,1024]{2,1,0:T(8,128)S(1)}, u32[]{:S(2)}, u32[]{:S(2)}) %collective-permute-start.7) | collective-permute-done | bytes 524320 | tf_op jit(solution)/shard_map/ppermute | solution.py:15
  70.2 0.8 constant_dynamic-update-slice_fusion
  71.1 6.6 %gather_fusion = f32[16,128,1024]{2,1,0:T(8,128)} fusion(f32[8,128,1024]{2,1,0:T(8,128)} %constant_dynamic-update-slice_fusion, s32[1024]{0:T(1024)S(1)} %pad_clamp_fusion), kind=kCustom, calls=%fused_computation | custom fusion | bytes 16777280 | tf_op jit(solution)/shard_map/gather | solution.py:30
  77.7 7.4 %fusion.17 = (f32[4,128,1024]{2,1,0:T(8,128)S(1)}, f32[4,128,1024]{2,1,0:T(8,128)S(1)}) fusion(f32[4,128,1024]{2,1,0:T(8,128)S(1)} %bitcast.53, f32[4,4,128,1024]{3,2,1,0:T(8,128)} %bitcast.48, f32[4,4,128,128]{3,2,1,0:T(8,128)S(1)} %copy-done.4, f32[4,4]{1,0:T(4,128)S(1)} %fusion.15), kind=kOutput, calls=%fused_computation.43 | convolution fusion | flops 3222536192 | bytes 15728704 | tf_op jit(solution)/shard_map/bkij,bkjd->bid/dot_general | solution.py:33
  85.1 9.6 %fusion.6 = f32[512,1024]{1,0:T(8,128)} fusion(f32[4,128,1024]{2,1,0:T(8,128)S(1)} %get-tuple-element.103, f32[512,1024]{1,0:T(8,128)S(1)} %bitcast.52, f32[1,1024,1024]{2,1,0:T(8,128)S(1)} %copy-done, f32[]{:T(128)S(6)} %log.4, f32[]{:T(128)S(6)} %sub.4, f32[1,512,1024]{2,1,0:T(8,128)} %param.9), kind=kOutput, calls=%fused_computation.11 | convolution fusion | flops 6445596672 | bytes 12582920 | tf_op jit(solution)/shard_map/dot_general | solution.py:38
  94.7 1.9 collective-permute-start.8
  96.6 3.5 %collective-permute-start.13 = (f32[512,1024]{1,0:T(8,128)}, f32[512,1024]{1,0:T(8,128)}, u32[]{:S(2)}, u32[]{:S(2)}) collective-permute-start(f32[512,1024]{1,0:T(8,128)} %bitcast.13), channel_id=1, source_target_pairs={{0,32},{32,64},{64,96},{96,128},{128,160},{160,192},{192,224},{1,3... | collective-permute-start | bytes 6291464 | tf_op jit(solution)/shard_map/ppermute | solution.py:15
  100.1 22.2 %collective-permute-done.8 = f32[512,1024]{1,0:T(8,128)} collective-permute-done((f32[512,1024]{1,0:T(8,128)}, f32[512,1024]{1,0:T(8,128)}, u32[]{:S(2)}, u32[]{:S(2)}) %collective-permute-start.8) | collective-permute-done | bytes 2097184 | tf_op jit(solution)/shard_map/ppermute | solution.py:15
  122.3 2.0 %broadcast_select_fusion = f32[512,1024]{1,0:T(8,128)S(1)} fusion(f32[512,1024]{1,0:T(8,128)S(1)} %copy-done.3, f32[512,1024]{1,0:T(8,128)} %collective-permute-done.8, pred[]{:T(512)S(6)} %eq.3), kind=kLoop, calls=%fused_computation.15 | loop fusion | flops 524288 | bytes 6291457 | tf_op jit(solution)/shard_map/jit(_where)/select_n | solution.py:69
  124.3 0.2 constant_dynamic-slice_fusion
  124.6 1.9 collective-permute-start.9
  126.5 3.9 %collective-permute-start.10 = (f32[1,128,1024]{2,1,0:T(8,128)S(1)}, f32[1,128,1024]{2,1,0:T(8,128)S(1)}, u32[]{:S(2)}, u32[]{:S(2)}) collective-permute-start(f32[1,128,1024]{2,1,0:T(8,128)S(1)} %get-tuple-element.92), channel_id=1, source_target_pairs={{1,0},{2,1},{3,2},{4,3},{5,4},{6,5},{7,6},{8,7},{9,8},{10,9},{11,1... | collective-permute-start | bytes 1572872 | tf_op jit(solution)/shard_map/ppermute | solution.py:15
  130.4 6.9 %collective-permute-start.11 = (f32[1,128,1024]{2,1,0:T(8,128)S(1)}, f32[1,128,1024]{2,1,0:T(8,128)S(1)}, u32[]{:S(2)}, u32[]{:S(2)}) collective-permute-start(f32[1,128,1024]{2,1,0:T(8,128)S(1)} %get-tuple-element.91), channel_id=1, source_target_pairs={{0,2},{1,3},{2,4},{3,5},{4,6},{5,7},{6,8},{7,9},{8,10},{9,11},{10,... | collective-permute-start | bytes 1572872 | tf_op jit(solution)/shard_map/ppermute | solution.py:15
  137.3 2.1 %collective-permute-start.12 = (f32[1,128,1024]{2,1,0:T(8,128)S(1)}, f32[1,128,1024]{2,1,0:T(8,128)S(1)}, u32[]{:S(2)}, u32[]{:S(2)}) collective-permute-start(f32[1,128,1024]{2,1,0:T(8,128)S(1)} %get-tuple-element.90), channel_id=1, source_target_pairs={{2,0},{3,1},{4,2},{5,3},{6,4},{7,5},{8,6},{9,7},{10,8},{11,9},{12,... | collective-permute-start | bytes 1572872 | tf_op jit(solution)/shard_map/ppermute | solution.py:15
  139.4 1.5 constant_dynamic-update-slice_fusion.9
  141.0 4.2 %collective-permute-done.9 = f32[1,128,1024]{2,1,0:T(8,128)S(1)} collective-permute-done((f32[1,128,1024]{2,1,0:T(8,128)S(1)}, f32[1,128,1024]{2,1,0:T(8,128)S(1)}, u32[]{:S(2)}, u32[]{:S(2)}) %collective-permute-start.9) | collective-permute-done | bytes 524320 | tf_op jit(solution)/shard_map/ppermute | solution.py:15
  145.1 0.8 constant_dynamic-update-slice_fusion.8
  146.0 0.4 collective-permute-done.10
  146.4 0.8 constant_dynamic-update-slice_fusion.7
  147.2 5.6 %collective-permute-done.11 = f32[1,128,1024]{2,1,0:T(8,128)S(1)} collective-permute-done((f32[1,128,1024]{2,1,0:T(8,128)S(1)}, f32[1,128,1024]{2,1,0:T(8,128)S(1)}, u32[]{:S(2)}, u32[]{:S(2)}) %collective-permute-start.11) | collective-permute-done | bytes 524320 | tf_op jit(solution)/shard_map/ppermute | solution.py:15
  152.8 0.8 constant_dynamic-update-slice_fusion.6
  153.6 14.9 %collective-permute-done.12 = f32[1,128,1024]{2,1,0:T(8,128)S(1)} collective-permute-done((f32[1,128,1024]{2,1,0:T(8,128)S(1)}, f32[1,128,1024]{2,1,0:T(8,128)S(1)}, u32[]{:S(2)}, u32[]{:S(2)}) %collective-permute-start.12) | collective-permute-done | bytes 524320 | tf_op jit(solution)/shard_map/ppermute | solution.py:15
  168.5 0.8 constant_dynamic-update-slice_fusion.5
  169.4 6.5 %gather_fusion.1 = f32[16,128,1024]{2,1,0:T(8,128)} fusion(f32[8,128,1024]{2,1,0:T(8,128)} %constant_dynamic-update-slice_fusion.5, s32[1024]{0:T(1024)S(1)} %pad_clamp_fusion), kind=kCustom, calls=%fused_computation.1 | custom fusion | bytes 16777280 | tf_op jit(solution)/shard_map/gather | solution.py:30
  175.9 7.1 %bitcast_multiply_fusion = f32[4,128,1024]{2,1,0:T(8,128)S(1)} fusion(f32[4,4,128,1024]{3,2,1,0:T(8,128)} %bitcast.49, f32[4,4,128,128]{3,2,1,0:T(8,128)S(1)} %copy-done.4, f32[4,4]{1,0:T(4,128)S(1)} %fusion.15), kind=kOutput, calls=%fused_computation.7 | convolution fusion | flops 3222011904 | bytes 11534400 | tf_op jit(solution)/shard_map/bkij,bkjd->bid/dot_general | solution.py:33
  183.0 2.4 %bitcast_add_fusion = f32[512,1024]{1,0:T(8,128)S(1)} fusion(f32[4,128,1024]{2,1,0:T(8,128)S(1)} %bitcast_multiply_fusion, f32[512,1024]{1,0:T(8,128)S(1)} %copy-done.3, f32[512,1024]{1,0:T(8,128)} %collective-permute-done.13, pred[]{:T(512)S(6)} %eq.3), kind=kLoop, calls=%fused_computation.6 | loop fusion | flops 1572864 | bytes 8388609 | tf_op jit(solution)/shard_map/add | solution.py:36
  185.4 0.4 copy-done.1
  185.8 8.3 %maximum_bitcast_fusion = f32[1,512,1024]{2,1,0:T(8,128)} fusion(f32[512,1024]{1,0:T(8,128)S(1)} %bitcast_add_fusion, f32[1,1024,1024]{2,1,0:T(8,128)S(1)} %copy-done.1, f32[]{:T(128)S(6)} %log.4, f32[]{:T(128)S(6)} %sub.4), kind=kOutput, calls=%fused_computation.13 | convolution fusion | flops 6444548096 | bytes 8388616 | tf_op jit(solution)/shard_map/dot_general | solution.py:38
  (20 shorter events, 0.1 us)
Async XLA Ops:
  2.1 16.1 %collective-permute-start = (s32[1]{0:T(128)}, s32[1]{0:T(128)}, u32[]{:S(2)}, u32[]{:S(2)}) collective-permute-start(s32[1]{0:T(128)} %bitcast.1), channel_id=1, source_target_pairs={{1,0},{2,1},{3,2},{4,3},{5,4},{6,5},{7,6},{8,7},{9,8},{10,9},{11,1... | collective-permute-start | bytes 20 | tf_op jit(solution)/shard_map/ppermute | solution.py:15
  4.1 15.5 %collective-permute-start.2 = (s32[1]{0:T(128)}, s32[1]{0:T(128)}, u32[]{:S(2)}, u32[]{:S(2)}) collective-permute-start(s32[1]{0:T(128)} %bitcast.3), channel_id=1, source_target_pairs={{0,1},{1,2},{2,3},{3,4},{4,5},{5,6},{6,7},{7,8},{8,9},{9,10},{10,1... | collective-permute-start | bytes 20 | tf_op jit(solution)/shard_map/ppermute | solution.py:15
  7.9 12.8 %collective-permute-start.4 = (s32[1]{0:T(128)}, s32[1]{0:T(128)}, u32[]{:S(2)}, u32[]{:S(2)}) collective-permute-start(s32[1]{0:T(128)} %bitcast.5), channel_id=1, source_target_pairs={{2,0},{3,1},{4,2},{5,3},{6,4},{7,5},{8,6},{9,7},{10,8},{11,9},{12,... | collective-permute-start | bytes 20 | tf_op jit(solution)/shard_map/ppermute | solution.py:15
  13.2 12.7 %copy-start.2 = (f32[1,512,1024]{2,1,0:T(8,128)S(1)}, f32[1,512,1024]{2,1,0:T(8,128)}, u32[]{:S(2)}) copy-start(f32[1,512,1024]{2,1,0:T(8,128)} %param.8) | copy-start | bytes 6291460
  13.3 8.9 %collective-permute-start.6 = (s32[1]{0:T(128)}, s32[1]{0:T(128)}, u32[]{:S(2)}, u32[]{:S(2)}) collective-permute-start(s32[1]{0:T(128)} %bitcast.7), channel_id=1, source_target_pairs={{0,2},{1,3},{2,4},{3,5},{4,6},{5,7},{6,8},{7,9},{8,10},{9,11},{10,... | collective-permute-start | bytes 20 | tf_op jit(solution)/shard_map/ppermute | solution.py:15
  26.0 5.9 %copy-start.5 = (s32[4,4]{1,0:T(4,128)S(1)}, s32[4,4]{1,0:T(4,128)}, u32[]{:S(2)}) copy-start(s32[4,4]{1,0:T(4,128)} %param.13) | copy-start | bytes 196
  26.0 9.3 %copy-start.6 = (s32[4]{0:T(128)S(1)}, s32[4]{0:T(128)}, u32[]{:S(2)}) copy-start(s32[4]{0:T(128)} %param.14) | copy-start | bytes 52
  27.2 22.5 %collective-permute-start.1 = (f32[1,128,1024]{2,1,0:T(8,128)}, f32[1,128,1024]{2,1,0:T(8,128)S(1)}, u32[]{:S(2)}, u32[]{:S(2)}) collective-permute-start(f32[1,128,1024]{2,1,0:T(8,128)} %get-tuple-element.97), channel_id=1, source_target_pairs={{0,1},{1,2},{2,3},{3,4},{4,5},{5,6},{6,7},{7,8},{8,9},{9,10},{10,1... | collective-permute-start | bytes 1572872 | tf_op jit(solution)/shard_map/ppermute | solution.py:15
  32.1 18.7 %collective-permute-start.3 = (f32[1,128,1024]{2,1,0:T(8,128)}, f32[1,128,1024]{2,1,0:T(8,128)S(1)}, u32[]{:S(2)}, u32[]{:S(2)}) collective-permute-start(f32[1,128,1024]{2,1,0:T(8,128)} %get-tuple-element.96), channel_id=1, source_target_pairs={{1,0},{2,1},{3,2},{4,3},{5,4},{6,5},{7,6},{8,7},{9,8},{10,9},{11,1... | collective-permute-start | bytes 1572872 | tf_op jit(solution)/shard_map/ppermute | solution.py:15
  35.4 30.3 %collective-permute-start.5 = (f32[1,128,1024]{2,1,0:T(8,128)}, f32[1,128,1024]{2,1,0:T(8,128)S(1)}, u32[]{:S(2)}, u32[]{:S(2)}) collective-permute-start(f32[1,128,1024]{2,1,0:T(8,128)} %get-tuple-element.95), channel_id=1, source_target_pairs={{0,2},{1,3},{2,4},{3,5},{4,6},{5,7},{6,8},{7,9},{8,10},{9,11},{10,... | collective-permute-start | bytes 1572872 | tf_op jit(solution)/shard_map/ppermute | solution.py:15
  39.4 30.9 %collective-permute-start.7 = (f32[1,128,1024]{2,1,0:T(8,128)S(1)}, f32[1,128,1024]{2,1,0:T(8,128)S(1)}, u32[]{:S(2)}, u32[]{:S(2)}) collective-permute-start(f32[1,128,1024]{2,1,0:T(8,128)S(1)} %get-tuple-element.94), channel_id=1, source_target_pairs={{2,0},{3,1},{4,2},{5,3},{6,4},{7,5},{8,6},{9,7},{10,8},{11,9},{12,... | collective-permute-start | bytes 1572872 | tf_op jit(solution)/shard_map/ppermute | solution.py:15
  71.1 6.6 %copy-start.4 = (f32[4,4,128,128]{3,2,1,0:T(8,128)S(1)}, f32[4,4,128,128]{3,2,1,0:T(8,128)}, u32[]{:S(2)}) copy-start(f32[4,4,128,128]{3,2,1,0:T(8,128)} %param.15) | copy-start | bytes 3145732
  77.7 7.4 %copy-start = (f32[1,1024,1024]{2,1,0:T(8,128)S(1)}, f32[1,1024,1024]{2,1,0:T(8,128)}, u32[]{:S(2)}) copy-start(f32[1,1024,1024]{2,1,0:T(8,128)} %param.11) | copy-start | bytes 12582916
  85.1 37.2 %copy-start.3 = (f32[512,1024]{1,0:T(8,128)S(1)}, f32[512,1024]{1,0:T(8,128)}, u32[]{:S(2)}) copy-start(f32[512,1024]{1,0:T(8,128)} %param.10) | copy-start | bytes 6291460
  94.7 27.7 %collective-permute-start.8 = (f32[512,1024]{1,0:T(8,128)}, f32[512,1024]{1,0:T(8,128)}, u32[]{:S(2)}, u32[]{:S(2)}) collective-permute-start(f32[512,1024]{1,0:T(8,128)} %fusion.6), channel_id=1, source_target_pairs={{0,32},{32,64},{64,96},{96,128},{128,160},{160,192},{192,224},{1,3... | collective-permute-start | bytes 6291464 | tf_op jit(solution)/shard_map/ppermute | solution.py:15
  96.6 86.4 %collective-permute-start.13 = (f32[512,1024]{1,0:T(8,128)}, f32[512,1024]{1,0:T(8,128)}, u32[]{:S(2)}, u32[]{:S(2)}) collective-permute-start(f32[512,1024]{1,0:T(8,128)} %bitcast.13), channel_id=1, source_target_pairs={{0,32},{32,64},{64,96},{96,128},{128,160},{160,192},{192,224},{1,3... | collective-permute-start | bytes 6291464 | tf_op jit(solution)/shard_map/ppermute | solution.py:15
  124.6 20.6 %collective-permute-start.9 = (f32[1,128,1024]{2,1,0:T(8,128)S(1)}, f32[1,128,1024]{2,1,0:T(8,128)S(1)}, u32[]{:S(2)}, u32[]{:S(2)}) collective-permute-start(f32[1,128,1024]{2,1,0:T(8,128)S(1)} %get-tuple-element.93), channel_id=1, source_target_pairs={{0,1},{1,2},{2,3},{3,4},{4,5},{5,6},{6,7},{7,8},{8,9},{9,10},{10,1... | collective-permute-start | bytes 1572872 | tf_op jit(solution)/shard_map/ppermute | solution.py:15
  126.5 19.9 %collective-permute-start.10 = (f32[1,128,1024]{2,1,0:T(8,128)S(1)}, f32[1,128,1024]{2,1,0:T(8,128)S(1)}, u32[]{:S(2)}, u32[]{:S(2)}) collective-permute-start(f32[1,128,1024]{2,1,0:T(8,128)S(1)} %get-tuple-element.92), channel_id=1, source_target_pairs={{1,0},{2,1},{3,2},{4,3},{5,4},{6,5},{7,6},{8,7},{9,8},{10,9},{11,1... | collective-permute-start | bytes 1572872 | tf_op jit(solution)/shard_map/ppermute | solution.py:15
  130.4 22.3 %collective-permute-start.11 = (f32[1,128,1024]{2,1,0:T(8,128)S(1)}, f32[1,128,1024]{2,1,0:T(8,128)S(1)}, u32[]{:S(2)}, u32[]{:S(2)}) collective-permute-start(f32[1,128,1024]{2,1,0:T(8,128)S(1)} %get-tuple-element.91), channel_id=1, source_target_pairs={{0,2},{1,3},{2,4},{3,5},{4,6},{5,7},{6,8},{7,9},{8,10},{9,11},{10,... | collective-permute-start | bytes 1572872 | tf_op jit(solution)/shard_map/ppermute | solution.py:15
  137.3 31.2 %collective-permute-start.12 = (f32[1,128,1024]{2,1,0:T(8,128)S(1)}, f32[1,128,1024]{2,1,0:T(8,128)S(1)}, u32[]{:S(2)}, u32[]{:S(2)}) collective-permute-start(f32[1,128,1024]{2,1,0:T(8,128)S(1)} %get-tuple-element.90), channel_id=1, source_target_pairs={{2,0},{3,1},{4,2},{5,3},{6,4},{7,5},{8,6},{9,7},{10,8},{11,9},{12,... | collective-permute-start | bytes 1572872 | tf_op jit(solution)/shard_map/ppermute | solution.py:15
  183.0 2.8 %copy-start.1 = (f32[1,1024,1024]{2,1,0:T(8,128)S(1)}, f32[1,1024,1024]{2,1,0:T(8,128)}, u32[]{:S(2)}) copy-start(f32[1,1024,1024]{2,1,0:T(8,128)} %param.11) | copy-start | bytes 12582916
where the time goes:
time: 195 us; the launch traced here: 194 us
  waiting for transfers between devices  68.6 us (35%)
  starting transfers between devices  50.2 us (26%)
  matrix products  32.3 us (17%)
  local copies, waits for them, and re-layouts  28 us (14%)
  between operations  8.69 us (4%)
  other arithmetic  6.29 us (3%)
    ppermute x14, waiting for transfers between devices, from_behind(): return lax.ppermute(value, axis, pairs)  68.6 us
    ppermute x14, starting transfers between devices, from_behind(): return lax.ppermute(value, axis, pairs)  50.2 us
    dot_general x2, matrix products, local_layer(): jnp.dot(mixed, weight, precision=lax.Precision.HIGHEST, preferred_element...  17.9 us
    dot_general x2, matrix products, local_layer(): jnp.einsum('bkij,bkjd->bid', values, selected, precision=lax.Precision.HI...  14.4 us
    gather x2, local copies, waits for them, and re-layouts, local_layer(): selected = sources[adj_slot]  13.1 us
    unnamed x22, local copies, waits for them, and re-layouts  10.2 us
  transfers between devices with their start and end apart: 14, of which 9 were waited for; matrix products, arithmetic and copies ran while one was open for 15% of the time, Pallas kernels for 0%

commit v1 on v0

v1 whole, which is shorter than its diff:
```python
import functools
import math

import jax
import jax.numpy as jnp
from jax import lax
from jax.experimental import pallas as pl
from jax.experimental.pallas import tpu as pltpu
from jax.sharding import PartitionSpec as P

MESH = pl.DeviceIdType.MESH
F32 = jnp.float32
BF16 = jnp.bfloat16
D = 1024
BLK = 128
NB = 4
KMAX = 4
V = NB * BLK
OFFSETS = (1, -1, 2, -2)
NJ = len(OFFSETS)
NC = 4
CW = D // NC
ORDER = (2, 3, 0, 1)


def split(x):
    hi = x.astype(BF16)
    return hi, (x - hi.astype(F32)).astype(BF16)


def dot(a, b):
    return jnp.dot(a, b, preferred_element_type=F32)


def kernel(
    n_seg, n_graph,
    slot, count, state, initial, fresh, weights, vals, wants,
    handed, advanced,
    state_v, vals_v, w_v, init_v, init_in, stage1, stage2, recv1, recv2,
    a_hi, a_lo, w_hi, w_lo, z, acc, out2, wants_in, *rest,
):
    h_in, h_out = rest[:NC], rest[NC : 2 * NC]
    (load_sem, want_send, want_recv, z_send, z_recv, x_send, h_recv, init_sem, init_recv, out_sem, adv_sem) = rest[2 * NC :]
    sec = lax.axis_index("segment")
    part = lax.axis_index("graph")
    first, last = sec == 0, sec == n_seg - 1
    dests = [part + o for o in OFFSETS]
    sources = [part - o for o in OFFSETS]
    has_dest = [(d >= 0) & (d < n_graph) for d in dests]
    has_source = [(d >= 0) & (d < n_graph) for d in sources]

    def cols(c):
        return pl.ds(c * CW, CW)

    loads = [
        pltpu.make_async_copy(src, dst, load_sem.at[i])
        for i, (src, dst) in enumerate(
            ((state, state_v), (vals, vals_v), (weights, w_v), (initial, init_v))
        )
    ]
    for load in loads:
        load.start()

    barrier = pltpu.get_barrier_semaphore()
    expected = jnp.int32(0)
    for d, ok in zip(dests, has_dest):
        @pl.when(ok)
        def _():
            pl.semaphore_signal(barrier, inc=1, device_id={"graph": d}, device_id_type=MESH)
        expected += ok.astype(jnp.int32)

    @pl.when(jnp.logical_not(last))
    def _():
        pl.semaphore_signal(barrier, inc=1, device_id={"segment": sec + 1}, device_id_type=MESH)

    @pl.when(jnp.logical_not(first))
    def _():
        pl.semaphore_signal(barrier, inc=1, device_id={"segment": sec - 1}, device_id_type=MESH)

    expected += jnp.logical_not(last).astype(jnp.int32) + jnp.logical_not(first).astype(jnp.int32)
    pl.semaphore_wait(barrier, expected)

    def want_copy(j):
        return pltpu.make_async_remote_copy(
            src_ref=wants, dst_ref=wants_in.at[j], send_sem=want_send.at[j], recv_sem=want_recv.at[j],
            device_id={"graph": sources[j]}, device_id_type=MESH,
        )

    def init_copy():
        return pltpu.make_async_remote_copy(
            src_ref=initial, dst_ref=init_in, send_sem=init_sem, recv_sem=init_recv,
            device_id={"segment": sec + 1}, device_id_type=MESH,
        )

    for j in ORDER:
        @pl.when(has_source[j])
        def _():
            want_copy(j).start()

    @pl.when(jnp.logical_not(last))
    def _():
        init_copy().start()

    @pl.when(first)
    def _():
        pltpu.make_async_copy(fresh, init_in, init_recv).start()
        for c in range(NC):
            pltpu.make_async_copy(fresh.at[:, :, cols(c)], h_in[c], h_recv.at[c]).start()

    loads[1].wait()

    def build(b, carry):
        for s in range(NB + NJ):
            tile = jnp.zeros((BLK, BLK), F32)
            for k in range(KMAX):
                live = ((slot[b, k] == s) & (k < count[b])).astype(jnp.int32)
                tile += live.astype(F32) * vals_v[b, k]
            hi, lo = split(0.9 * tile)
            rows = pl.ds(pl.multiple_of(b * BLK, BLK), BLK)
            a_hi[rows, pl.ds(s * BLK, BLK)] = hi
            a_lo[rows, pl.ds(s * BLK, BLK)] = lo
        return carry

    lax.fori_loop(0, NB, build, 0)

    loads[0].wait()
    for j in ORDER:
        @pl.when(has_dest[j])
        def _():
            want_copy(j).wait_recv()

        @pl.when(jnp.logical_not(has_source[j]))
        def _():
            recv1[j] = jnp.zeros((NC, BLK, CW), F32)
            recv2[j] = jnp.zeros((NC, BLK, CW), F32)

    def block_copy(tick, j, c):
        return pltpu.make_async_remote_copy(
            src_ref=(stage1, stage2)[tick].at[j, c], dst_ref=(recv1, recv2)[tick].at[j, c],
            send_sem=z_send.at[tick, j, c], recv_sem=z_recv.at[tick, j, c],
            device_id={"graph": dests[j]}, device_id_type=MESH,
        )

    def send_blocks(tick, c):
        for j in ORDER:
            @pl.when(has_dest[j])
            def _():
                block = wants_in[j, j]
                if tick == 0:
                    stage1[j, c] = state_v[block, :, cols(c)]
                else:
                    stage2[j, c] = h_in[c][block]
                block_copy(tick, j, c).start()

    for c in range(NC):
        send_blocks(0, c)

    beta = jnp.float32(0.0)
    for s in range(n_seg):
        beta = jnp.where(sec == s, jnp.float32(math.log(0.5 / (s + 1.0) + 1.0)), beta)
    loads[2].wait()

    def fold(i, carry):
        rows = pl.ds(pl.multiple_of(i * BLK, BLK), BLK)
        r = lax.broadcasted_iota(jnp.int32, (BLK, D), 0) + i * BLK
        q = lax.broadcasted_iota(jnp.int32, (BLK, D), 1)
        w = beta * w_v[rows, :] + jnp.where(r == q, 1.0 - beta, 0.0)
        w_hi[rows, :], w_lo[rows, :] = split(w)
        return carry

    lax.fori_loop(0, D // BLK, fold, 0)

    def aggregate(lo_col, feats):
        hi, lo = split(feats)
        k = pl.ds(lo_col, NB * BLK)
        return dot(a_hi[:, k], hi) + dot(a_lo[:, k], hi) + dot(a_hi[:, k], lo)

    def own_part(feats, first_feats, c):
        z[c] = aggregate(0, feats) + 0.1 * first_feats

    def rest_part(tick, c, finish):
        for j in ORDER:
            @pl.when(has_source[j])
            def _():
                block_copy(tick, j, c).wait_recv()
        recv = (recv1, recv2)[tick]
        zc = z[c] + aggregate(V, recv[:, c].reshape(V, CW))
        hi, lo = split(zc)
        for n in range(NC):
            part_n = dot(hi, w_hi[cols(c), cols(n)]) + dot(lo, w_hi[cols(c), cols(n)]) + dot(hi, w_lo[cols(c), cols(n)])
            if c > 0:
                part_n += acc[n]
            if c < NC - 1:
                acc[n] = part_n
            else:
                finish(n, jnp.maximum(part_n, 0.0))

    loads[3].wait()
    for c in range(NC):
        own_part(state_v[:, :, cols(c)].reshape(V, CW), init_v[:, :, cols(c)].reshape(V, CW), c)

    def hand_copy(n):
        return pltpu.make_async_remote_copy(
            src_ref=h_out[n], dst_ref=h_in[n], send_sem=x_send.at[n], recv_sem=h_recv.at[n],
            device_id={"segment": sec + 1}, device_id_type=MESH,
        )

    def hand_store(n):
        return pltpu.make_async_copy(h_out[n], handed.at[:, :, cols(n)], out_sem.at[n])

    def finish_first(n, value):
        h_out[n][...] = value.reshape(NB, BLK, CW)

        @pl.when(jnp.logical_not(last))
        def _():
            hand_copy(n).start()
        hand_store(n).start()

    for c in range(NC):
        rest_part(0, c, finish_first)

    def take(c):
        pltpu.make_async_copy(h_in[c], h_in[c], h_recv.at[c]).wait()
        send_blocks(1, c)
        if c == 0:
            pltpu.make_async_copy(init_in, init_in, init_recv).wait()
        own_part(h_in[c][...].reshape(V, CW), init_in[:, :, cols(c)].reshape(V, CW), c)

    def adv_store(n):
        return pltpu.make_async_copy(out2.at[n], advanced.at[:, :, cols(n)], adv_sem.at[n])

    def finish_second(n, value):
        out2[n] = value.reshape(NB, BLK, CW)
        adv_store(n).start()

    take(0)
    for c in range(NC):
        if c + 1 < NC:
            take(c + 1)
        rest_part(1, c, finish_second)

    for j in range(NJ):
        @pl.when(has_source[j])
        def _():
            want_copy(j).wait_send()

        @pl.when(has_dest[j])
        def _():
            for tick in range(2):
                for c in range(NC):
                    block_copy(tick, j, c).wait_send()

    @pl.when(jnp.logical_not(last))
    def _():
        init_copy().wait_send()
        for n in range(NC):
            hand_copy(n).wait_send()

    for n in range(NC):
        hand_store(n).wait()
        adv_store(n).wait()


def blocks(x):
    return x.reshape(NB, BLK, D)


def shards(n_seg, n_graph, state, initial, fresh, weights, wants, adj_slot, adj_count, adj_vals):
    smem = pl.BlockSpec(memory_space=pltpu.SMEM)
    hbm = pl.BlockSpec(memory_space=pl.ANY)
    out = jax.ShapeDtypeStruct((NB, BLK, D), F32)
    dma = pltpu.SemaphoreType.DMA
    handed, advanced = pl.pallas_call(
        functools.partial(kernel, n_seg, n_graph),
        out_shape=(out, out),
        in_specs=[smem, smem] + [hbm] * 5 + [smem],
        out_specs=(hbm, hbm),
        scratch_shapes=[
            pltpu.VMEM((NB, BLK, D), F32),
            pltpu.VMEM((NB, KMAX, BLK, BLK), F32),
            pltpu.VMEM((D, D), F32),
            pltpu.VMEM((NB, BLK, D), F32),
            pltpu.VMEM((NB, BLK, D), F32),
            pltpu.VMEM((NJ, NC, BLK, CW), F32),
            pltpu.VMEM((NJ, NC, BLK, CW), F32),
            pltpu.VMEM((NJ, NC, BLK, CW), F32),
            pltpu.VMEM((NJ, NC, BLK, CW), F32),
            pltpu.VMEM((V, (NB + NJ) * BLK), BF16),
            pltpu.VMEM((V, (NB + NJ) * BLK), BF16),
            pltpu.VMEM((D, D), BF16),
            pltpu.VMEM((D, D), BF16),
            pltpu.VMEM((NC, V, CW), F32),
            pltpu.VMEM((NC, V, CW), F32),
            pltpu.VMEM((NC, NB, BLK, CW), F32),
            pltpu.SMEM((NJ, NJ), jnp.int32),
        ]
        + [pltpu.VMEM((NB, BLK, CW), F32) for _ in range(2 * NC)]
        + [
            dma((4,)), dma((NJ,)), dma((NJ,)), dma((2, NJ, NC)), dma((2, NJ, NC)),
            dma((NC,)), dma((NC,)), dma, dma, dma((NC,)), dma((NC,)),
        ],
        compiler_params=pltpu.CompilerParams(
            collective_id=0, has_side_effects=True, vmem_limit_bytes=60 * 1024 * 1024
        ),
    )(
        adj_slot, adj_count, blocks(state), blocks(initial), blocks(fresh), weights[0], adj_vals, wants.reshape(NJ)
    )
    return handed.reshape(1, V, D), advanced.reshape(1, V, D)


def solution(mesh):
    return jax.shard_map(
        functools.partial(shards, mesh.shape["segment"], mesh.shape["graph"]),
        mesh=mesh,
        in_specs=(
            P("segment", "graph", None),
            P("segment", "graph", None),
            P("graph", None),
            P("segment", None, None),
            P("graph", None, None),
            P("graph", None),
            P("graph"),
            P("graph", None, None, None),
        ),
        out_specs=(P("segment", "graph", None), P("segment", "graph", None)),
        check_vma=False,
    )
```

time: 195 us -> 95.3 us (0.49)
  the two profiles are of different devices: /device:TPU:82 before, /device:TPU:25 now
where the time goes in v1:
time: 95.3 us; the launch traced here: 95.2 us
  Pallas kernels  89.9 us (94%)
  local copies, waits for them, and re-layouts  4.63 us (5%)
    pallas_call x1, Pallas kernels, shards(): pl.pallas_call(functools.partial(kernel, n_seg, n_graph), out_shape=(out,...  89.9 us
    unnamed x4, local copies, waits for them, and re-layouts  4.63 us

profile of v1, /device:TPU:25, one launch (start us, length us, event | category | flops | bytes accessed | tf_op | source)
XLA Modules:
  0.0 95.2 jit_solution(18297047226247648641)
XLA Ops:
  0.6 89.9 %shard_map.95 = (f32[4,128,1024]{2,1,0:T(8,128)}, f32[4,128,1024]{2,1,0:T(8,128)}) custom-call(s32[4,4]{1,0:T(4,128)} %slot.1, s32[4]{0:T(128)} %count.1, f32[4,128,1024]{2,1,0:T(8,128)} %bitcast.8, f32[4,128,1024]{2,1,0:T(8,128)} %bitcast.9, f32[4,128,1024]{2,1,0:T(8,128)} %bitcast.10, f32[1024,1024]{1,0:T(8,128)} %bitcast.7, f32[4,4,128,128]{3,2,1,0:T(8,128)} %vals.1, ...), custom_call_target="tpu_custom_call" | custom-call | tf_op jit(solution)/shard_map/pallas_call | solution.py:273
  90.6 0.0 copy-start
  90.6 3.3 %copy.12 = f32[1,512,1024]{2,1,0:T(8,128)} copy(f32[1,512,1024]{2,1,0:T(8,128)} %bitcast.12) | data formatting | bytes 4194304
  93.9 0.0 copy-done
  93.9 1.3 %copy.13 = f32[1,512,1024]{2,1,0:T(8,128)} copy(f32[1,512,1024]{2,1,0:T(8,128)S(1)} %bitcast.11) | data formatting | bytes 4194304
Async XLA Ops:
  90.6 3.3 %copy-start = (f32[4,128,1024]{2,1,0:T(8,128)S(1)}, f32[4,128,1024]{2,1,0:T(8,128)}, u32[]{:S(2)}) copy-start(f32[4,128,1024]{2,1,0:T(8,128)} %get-tuple-element.5) | copy-start | bytes 6291460

commit v2 on v1

v2 whole, which is shorter than its diff:
```python
import functools
import math

import jax
import jax.numpy as jnp
from jax import lax
from jax.experimental import pallas as pl
from jax.experimental.pallas import tpu as pltpu
from jax.sharding import PartitionSpec as P

MESH = pl.DeviceIdType.MESH
F32 = jnp.float32
BF16 = jnp.bfloat16
D = 1024
BLK = 128
NB = 4
KMAX = 4
V = NB * BLK
OFFSETS = (1, -1, 2, -2)
NJ = len(OFFSETS)
WIDTHS = (256, 256, 256, 128, 128)
NC = len(WIDTHS)
STARTS = tuple(sum(WIDTHS[:c]) for c in range(NC))
ORDER = (2, 3, 0, 1)
GO = 2


def split(x):
    hi = x.astype(BF16)
    return hi, (x - hi.astype(F32)).astype(BF16)


def dot(a, b):
    return jnp.dot(a, b, preferred_element_type=F32)


def kernel(
    n_seg, n_graph,
    slot_hbm, count_hbm, state, initial, fresh, weights, vals, wants_hbm,
    handed, advanced,
    state_v, vals_v, w_v, init_v, init_in,
    a_hi, a_lo, w_hi, w_lo, wants_in, slot, count, *rest,
):
    h_in, stage1, stage2, recv1, recv2, z, acc = (rest[i * NC : (i + 1) * NC] for i in range(7))
    (load_sem, want_send, want_recv, z_send, z_recv, x_send, h_recv, init_sem, init_recv, go_sem) = rest[7 * NC :]
    sec = lax.axis_index("segment")
    part = lax.axis_index("graph")
    first, last = sec == 0, sec == n_seg - 1
    odd = sec % 2 == 1
    dests = [part + o for o in OFFSETS]
    sources = [part - o for o in OFFSETS]
    has_dest = [(d >= 0) & (d < n_graph) for d in dests]
    has_source = [(d >= 0) & (d < n_graph) for d in sources]

    def cols(c):
        return pl.ds(STARTS[c], WIDTHS[c])

    loads = [
        pltpu.make_async_copy(src, dst, load_sem.at[i])
        for i, (src, dst) in enumerate(
            ((state, state_v), (vals, vals_v), (weights, w_v), (initial, init_v), (slot_hbm, slot), (count_hbm, count))
        )
    ]
    loads[0].start()

    barrier = pltpu.get_barrier_semaphore()
    expected = jnp.int32(0)
    for d, ok in zip(dests, has_dest):
        @pl.when(ok)
        def _():
            pl.semaphore_signal(barrier, inc=1, device_id={"graph": d}, device_id_type=MESH)
        expected += ok.astype(jnp.int32)

    @pl.when(jnp.logical_not(last))
    def _():
        pl.semaphore_signal(barrier, inc=1, device_id={"segment": sec + 1}, device_id_type=MESH)

    @pl.when(jnp.logical_not(first))
    def _():
        pl.semaphore_signal(barrier, inc=1, device_id={"segment": sec - 1}, device_id_type=MESH)

    expected += jnp.logical_not(last).astype(jnp.int32) + jnp.logical_not(first).astype(jnp.int32)
    pl.semaphore_wait(barrier, expected)

    def want_copy(j):
        return pltpu.make_async_remote_copy(
            src_ref=wants_hbm, dst_ref=wants_in.at[j], send_sem=want_send.at[j], recv_sem=want_recv.at[j],
            device_id={"graph": sources[j]}, device_id_type=MESH,
        )

    def init_copy():
        return pltpu.make_async_remote_copy(
            src_ref=initial, dst_ref=init_in, send_sem=init_sem, recv_sem=init_recv,
            device_id={"segment": sec + 1}, device_id_type=MESH,
        )

    for j in ORDER:
        @pl.when(has_source[j])
        def _():
            want_copy(j).start()

    for load in loads[1:]:
        load.start()

    @pl.when(jnp.logical_not(last))
    def _():
        init_copy().start()

    @pl.when(first)
    def _():
        pltpu.make_async_copy(fresh, init_in, init_recv).start()
        for c in range(NC):
            pltpu.make_async_copy(fresh.at[:, :, cols(c)], h_in[c], h_recv.at[c]).start()

    def block_copy(tick, j, c):
        return pltpu.make_async_remote_copy(
            src_ref=(stage1, stage2)[tick][c].at[j], dst_ref=(recv1, recv2)[tick][c].at[j],
            send_sem=z_send.at[tick, j, c], recv_sem=z_recv.at[tick, j, c],
            device_id={"graph": dests[j]}, device_id_type=MESH,
        )

    loads[0].wait()
    for c in range(NC):
        for j in ORDER:
            @pl.when(has_dest[j])
            def _():
                if c == 0:
                    want_copy(j).wait_recv()
                stage1[c][j] = state_v[wants_in[j, j], :, cols(c)]

                @pl.when(odd)
                def _():
                    block_copy(0, j, c).start()

    for j in ORDER:
        @pl.when(jnp.logical_not(has_source[j]))
        def _():
            for c in range(NC):
                recv1[c][j] = jnp.zeros((BLK, WIDTHS[c]), F32)
                recv2[c][j] = jnp.zeros((BLK, WIDTHS[c]), F32)

    loads[1].wait()
    loads[4].wait()
    loads[5].wait()

    def build(b, carry):
        for s in range(NB + NJ):
            tile = jnp.zeros((BLK, BLK), F32)
            for k in range(KMAX):
                live = ((slot[b, k] == s) & (k < count[b])).astype(jnp.int32)
                tile += live.astype(F32) * vals_v[b, k]
            hi, lo = split(0.9 * tile)
            rows = pl.ds(pl.multiple_of(b * BLK, BLK), BLK)
            a_hi[rows, pl.ds(s * BLK, BLK)] = hi
            a_lo[rows, pl.ds(s * BLK, BLK)] = lo
        return carry

    lax.fori_loop(0, NB, build, 0)

    beta = jnp.float32(0.0)
    for s in range(n_seg):
        beta = jnp.where(sec == s, jnp.float32(math.log(0.5 / (s + 1.0) + 1.0)), beta)
    loads[2].wait()

    def fold(i, carry):
        rows = pl.ds(pl.multiple_of(i * BLK, BLK), BLK)
        r = lax.broadcasted_iota(jnp.int32, (BLK, D), 0) + i * BLK
        q = lax.broadcasted_iota(jnp.int32, (BLK, D), 1)
        w = beta * w_v[rows, :] + jnp.where(r == q, 1.0 - beta, 0.0)
        w_hi[rows, :], w_lo[rows, :] = split(w)
        return carry

    lax.fori_loop(0, D // BLK, fold, 0)

    def aggregate(lo_col, feats):
        hi, lo = split(feats)
        k = pl.ds(lo_col, NB * BLK)
        return dot(a_hi[:, k], hi) + dot(a_lo[:, k], hi) + dot(a_hi[:, k], lo)

    def own_part(feats, first_feats, c):
        z[c][...] = aggregate(0, feats) + 0.1 * first_feats

    def rest_part(tick, c, finish):
        for j in ORDER:
            @pl.when(has_source[j])
            def _():
                block_copy(tick, j, c).wait_recv()
        recv = (recv1, recv2)[tick][c]
        if tick == 0 and c == GO:
            @pl.when(odd)
            def _():
                pl.semaphore_signal(go_sem, inc=1, device_id={"segment": sec - 1}, device_id_type=MESH)
        zc = z[c][...] + aggregate(V, recv[...].reshape(V, WIDTHS[c]))
        hi, lo = split(zc)
        for n in range(NC):
            part_n = dot(hi, w_hi[cols(c), cols(n)]) + dot(lo, w_hi[cols(c), cols(n)]) + dot(hi, w_lo[cols(c), cols(n)])
            if c > 0:
                part_n += acc[n][...]
            if c < NC - 1:
                acc[n][...] = part_n
            else:
                finish(n, jnp.maximum(part_n, 0.0))

    loads[3].wait()
    for c in range(NC):
        own_part(state_v[:, :, cols(c)].reshape(V, WIDTHS[c]), init_v[:, :, cols(c)].reshape(V, WIDTHS[c]), c)

    def hand_copy(n):
        return pltpu.make_async_remote_copy(
            src_ref=handed.at[:, :, cols(n)], dst_ref=h_in[n], send_sem=x_send.at[n], recv_sem=h_recv.at[n],
            device_id={"segment": sec + 1}, device_id_type=MESH,
        )

    def finish_first(n, value):
        handed[:, :, cols(n)] = value.reshape(NB, BLK, WIDTHS[n])

        @pl.when(jnp.logical_not(last))
        def _():
            hand_copy(n).start()

    @pl.when(jnp.logical_not(odd))
    def _():
        pl.semaphore_wait(go_sem, 1)
        for c in range(NC):
            for j in ORDER:
                @pl.when(has_dest[j])
                def _():
                    block_copy(0, j, c).start()

    def forward(c):
        pltpu.make_async_copy(h_in[c], h_in[c], h_recv.at[c]).wait()
        for j in ORDER:
            @pl.when(has_dest[j])
            def _():
                stage2[c][j] = h_in[c][wants_in[j, j]]
                block_copy(1, j, c).start()

    def early(c):
        @pl.when(jnp.logical_not(odd))
        def _():
            forward(c)

    for c in range(NC):
        rest_part(0, c, finish_first)
        if c == 0:
            early(0)
        if c == 2:
            early(1)

    @pl.when(odd)
    def _():
        forward(0)
        forward(1)
    for c in range(2, NC):
        forward(c)

    def finish_second(n, value):
        advanced[:, :, cols(n)] = value.reshape(NB, BLK, WIDTHS[n])

    pltpu.make_async_copy(init_in, init_in, init_recv).wait()
    for c in range(NC):
        own_part(h_in[c][...].reshape(V, WIDTHS[c]), init_in[:, :, cols(c)].reshape(V, WIDTHS[c]), c)
    for c in range(NC):
        rest_part(1, c, finish_second)

    for j in range(NJ):
        @pl.when(has_source[j])
        def _():
            want_copy(j).wait_send()

        @pl.when(has_dest[j])
        def _():
            for tick in range(2):
                for c in range(NC):
                    block_copy(tick, j, c).wait_send()

    @pl.when(jnp.logical_not(last))
    def _():
        init_copy().wait_send()
        for n in range(NC):
            hand_copy(n).wait_send()


def blocks(x):
    return x.reshape(NB, BLK, D)


def shards(n_seg, n_graph, state, initial, fresh, weights, wants, adj_slot, adj_count, adj_vals):
    smem = pl.BlockSpec(memory_space=pltpu.SMEM)
    hbm = pl.BlockSpec(memory_space=pltpu.HBM)
    vmem = pl.BlockSpec(memory_space=pltpu.VMEM)
    out = jax.ShapeDtypeStruct((NB, BLK, D), F32)
    dma = pltpu.SemaphoreType.DMA
    handed, advanced = pl.pallas_call(
        functools.partial(kernel, n_seg, n_graph),
        out_shape=(out, out),
        in_specs=[hbm] * 8,
        out_specs=(vmem, vmem),
        scratch_shapes=[
            pltpu.VMEM((NB, BLK, D), F32),
            pltpu.VMEM((NB, KMAX, BLK, BLK), F32),
            pltpu.VMEM((D, D), F32),
            pltpu.VMEM((NB, BLK, D), F32),
            pltpu.VMEM((NB, BLK, D), F32),
            pltpu.VMEM((V, (NB + NJ) * BLK), BF16),
            pltpu.VMEM((V, (NB + NJ) * BLK), BF16),
            pltpu.VMEM((D, D), BF16),
            pltpu.VMEM((D, D), BF16),
            pltpu.SMEM((NJ, NJ), jnp.int32),
            pltpu.SMEM((NB, KMAX), jnp.int32),
            pltpu.SMEM((NB,), jnp.int32),
        ]
        + [pltpu.VMEM((NB, BLK, w), F32) for _ in range(5) for w in WIDTHS]
        + [pltpu.VMEM((V, w), F32) for _ in range(2) for w in WIDTHS]
        + [
            dma((6,)), dma((NJ,)), dma((NJ,)), dma((2, NJ, NC)), dma((2, NJ, NC)),
            dma((NC,)), dma((NC,)), dma, dma,
            pltpu.SemaphoreType.REGULAR,
        ],
        compiler_params=pltpu.CompilerParams(
            collective_id=0, has_side_effects=True, vmem_limit_bytes=48 * 1024 * 1024
        ),
    )(
        *(
            pltpu.with_memory_space_constraint(x, pltpu.HBM)
            for x in (
                adj_slot, adj_count, blocks(state), blocks(initial), blocks(fresh), weights[0], adj_vals,
                wants.reshape(NJ),
            )
        )
    )
    return handed.reshape(1, V, D), advanced.reshape(1, V, D)


def solution(mesh):
    return jax.shard_map(
        functools.partial(shards, mesh.shape["segment"], mesh.shape["graph"]),
        mesh=mesh,
        in_specs=(
            P("segment", "graph", None),
            P("segment", "graph", None),
            P("graph", None),
            P("segment", None, None),
            P("graph", None, None),
            P("graph", None),
            P("graph"),
            P("graph", None, None, None),
        ),
        out_specs=(P("segment", "graph", None), P("segment", "graph", None)),
        check_vma=False,
    )
```

time: 95.3 us -> 85.8 us (0.900)
  Pallas kernels: 89.9 us -> 82.1 us
  local copies, waits for them, and re-layouts: 4.63 us -> 2.64 us
    pallas_call x1, Pallas kernels: 89.9 us -> 82.1 us  [shards(): pl.pallas_call(functools.partial(kernel, n_seg, n_graph), out_shape=(out,...]
    unnamed x4 -> x2, local copies, waits for them, and re-layouts: 4.63 us -> 2.64 us
where the time goes in v2:
time: 85.8 us; the launch traced here: 85.4 us
  Pallas kernels  82.1 us (96%)
  local copies, waits for them, and re-layouts  2.64 us (3%)
    pallas_call x1, Pallas kernels, shards(): pl.pallas_call(functools.partial(kernel, n_seg, n_graph), out_shape=(out,...  82.1 us
    unnamed x2, local copies, waits for them, and re-layouts  2.64 us

profile of v2, /device:TPU:25, one launch (start us, length us, event | category | flops | bytes accessed | tf_op | source)
XLA Modules:
  0.0 85.4 jit_solution(777559274709192222)
XLA Ops:
  0.6 82.1 %shard_map.95 = (f32[4,128,1024]{2,1,0:T(8,128)S(1)}, f32[4,128,1024]{2,1,0:T(8,128)S(1)}) custom-call(s32[4,4]{1,0:T(4,128)} %slot_hbm.1, s32[4]{0:T(128)} %count_hbm.1, f32[4,128,1024]{2,1,0:T(8,128)} %bitcast.10, f32[4,128,1024]{2,1,0:T(8,128)} %bitcast.11, f32[4,128,1024]{2,1,0:T(8,128)} %bitcast.12, f32[1024,1024]{1,0:T(8,128)} %bitcast.9, ...), custom_call_target="tpu_custom_call" | custom-call | tf_op jit(solution)/shard_map/pallas_call | solution.py:294
  82.8 1.3 %copy.12 = f32[1,512,1024]{2,1,0:T(8,128)} copy(f32[1,512,1024]{2,1,0:T(8,128)S(1)} %bitcast.8) | data formatting | bytes 4194304
  84.1 1.3 %copy.13 = f32[1,512,1024]{2,1,0:T(8,128)} copy(f32[1,512,1024]{2,1,0:T(8,128)S(1)} %bitcast.7) | data formatting | bytes 4194304

commit v3 on v2

--- a/solution.py
+++ b/solution.py
@@ -21,7 +21,7 @@
 WIDTHS = (256, 256, 256, 128, 128)
 NC = len(WIDTHS)
 STARTS = tuple(sum(WIDTHS[:c]) for c in range(NC))
-ORDER = (2, 3, 0, 1)
+ORDER = (0, 1, 2, 3)
 GO = 2
 
 
@@ -34,15 +34,35 @@
     return jnp.dot(a, b, preferred_element_type=F32)
 
 
+def adjacent(a_hi, a_lo, feats):
+    hi, lo = split(feats)
+    width = feats.shape[1]
+    if width > BLK:
+        return dot(a_hi, hi) + dot(a_lo, hi) + dot(a_hi, lo)
+    both = dot(a_hi, jnp.concatenate([hi, lo], axis=1))
+    return both[:, :width] + both[:, width:] + dot(a_lo, hi)
+
+
+def weighted(parts, w_hi, w_lo):
+    hi, lo = parts
+    if hi.shape[1] > BLK:
+        return dot(hi, w_hi) + dot(lo, w_hi) + dot(hi, w_lo)
+    return dot(jnp.concatenate([hi, lo], axis=1), jnp.concatenate([w_hi, w_hi], axis=0)) + dot(hi, w_lo)
+
+
+def cols(c):
+    return pl.ds(STARTS[c], WIDTHS[c])
+
+
 def kernel(
     n_seg, n_graph,
     slot_hbm, count_hbm, state, initial, fresh, weights, vals, wants_hbm,
-    handed, advanced,
-    state_v, vals_v, w_v, init_v, init_in,
-    a_hi, a_lo, w_hi, w_lo, wants_in, slot, count, *rest,
+    handed, acc, z_last, recv_last, a_hi, a_lo, w_hi, w_lo,
+    state_v, vals_v, w_v, init_v, init_in, wants_in, slot, count, *rest,
 ):
-    h_in, stage1, stage2, recv1, recv2, z, acc = (rest[i * NC : (i + 1) * NC] for i in range(7))
-    (load_sem, want_send, want_recv, z_send, z_recv, x_send, h_recv, init_sem, init_recv, go_sem) = rest[7 * NC :]
+    h_in, stage1, stage2, recv1, recv2, z = (rest[i * NC : (i + 1) * NC] for i in range(6))
+    recv2 = recv2[: NC - 1] + (recv_last,)
+    (load_sem, want_send, want_recv, z_send, z_recv, x_send, h_recv, init_recv, go_sem) = rest[6 * NC :]
     sec = lax.axis_index("segment")
     part = lax.axis_index("graph")
     first, last = sec == 0, sec == n_seg - 1
@@ -52,8 +72,7 @@
     has_dest = [(d >= 0) & (d < n_graph) for d in dests]
     has_source = [(d >= 0) & (d < n_graph) for d in sources]
 
-    def cols(c):
-        return pl.ds(STARTS[c], WIDTHS[c])
+    due = sum(ok.astype(jnp.int32) for ok in has_source)
 
     loads = [
         pltpu.make_async_copy(src, dst, load_sem.at[i])
@@ -90,7 +109,7 @@
 
     def init_copy():
         return pltpu.make_async_remote_copy(
-            src_ref=initial, dst_ref=init_in, send_sem=init_sem, recv_sem=init_recv,
+            src_ref=initial, dst_ref=init_in, send_sem=x_send, recv_sem=init_recv,
             device_id={"segment": sec + 1}, device_id_type=MESH,
         )
 
@@ -115,7 +134,7 @@
     def block_copy(tick, j, c):
         return pltpu.make_async_remote_copy(
             src_ref=(stage1, stage2)[tick][c].at[j], dst_ref=(recv1, recv2)[tick][c].at[j],
-            send_sem=z_send.at[tick, j, c], recv_sem=z_recv.at[tick, j, c],
+            send_sem=z_send.at[j], recv_sem=z_recv.at[tick, c],
             device_id={"graph": dests[j]}, device_id_type=MESH,
         )
 
@@ -173,31 +192,34 @@
     lax.fori_loop(0, D // BLK, fold, 0)
 
     def aggregate(lo_col, feats):
-        hi, lo = split(feats)
         k = pl.ds(lo_col, NB * BLK)
-        return dot(a_hi[:, k], hi) + dot(a_lo[:, k], hi) + dot(a_hi[:, k], lo)
+        return adjacent(a_hi[:, k], a_lo[:, k], feats)
 
     def own_part(feats, first_feats, c):
         z[c][...] = aggregate(0, feats) + 0.1 * first_feats
 
+    def arrive(tick, c):
+        ref = (recv1, recv2)[tick][c]
+        for blocks_due in range(2, NJ + 1):
+            @pl.when(due == blocks_due)
+            def _():
+                due_ref = ref.at[pl.ds(0, blocks_due)]
+                pltpu.make_async_copy(due_ref, due_ref, z_recv.at[tick, c]).wait()
+
     def rest_part(tick, c, finish):
-        for j in ORDER:
-            @pl.when(has_source[j])
-            def _():
-                block_copy(tick, j, c).wait_recv()
+        arrive(tick, c)
         recv = (recv1, recv2)[tick][c]
         if tick == 0 and c == GO:
             @pl.when(odd)
             def _():
                 pl.semaphore_signal(go_sem, inc=1, device_id={"segment": sec - 1}, device_id_type=MESH)
-        zc = z[c][...] + aggregate(V, recv[...].reshape(V, WIDTHS[c]))
-        hi, lo = split(zc)
+        zc = split(z[c][...] + aggregate(V, recv[...].reshape(V, WIDTHS[c])))
         for n in range(NC):
-            part_n = dot(hi, w_hi[cols(c), cols(n)]) + dot(lo, w_hi[cols(c), cols(n)]) + dot(hi, w_lo[cols(c), cols(n)])
+            part_n = weighted(zc, w_hi[cols(c), cols(n)], w_lo[cols(c), cols(n)])
             if c > 0:
-                part_n += acc[n][...]
+                part_n += acc[:, cols(n)]
             if c < NC - 1:
-                acc[n][...] = part_n
+                acc[:, cols(n)] = part_n
             else:
                 finish(n, jnp.maximum(part_n, 0.0))
 
@@ -207,7 +229,7 @@
 
     def hand_copy(n):
         return pltpu.make_async_remote_copy(
-            src_ref=handed.at[:, :, cols(n)], dst_ref=h_in[n], send_sem=x_send.at[n], recv_sem=h_recv.at[n],
+            src_ref=handed.at[:, :, cols(n)], dst_ref=h_in[n], send_sem=x_send, recv_sem=h_recv.at[n],
             device_id={"segment": sec + 1}, device_id_type=MESH,
         )
 
@@ -254,14 +276,13 @@
     for c in range(2, NC):
         forward(c)
 
-    def finish_second(n, value):
-        advanced[:, :, cols(n)] = value.reshape(NB, BLK, WIDTHS[n])
-
     pltpu.make_async_copy(init_in, init_in, init_recv).wait()
     for c in range(NC):
         own_part(h_in[c][...].reshape(V, WIDTHS[c]), init_in[:, :, cols(c)].reshape(V, WIDTHS[c]), c)
-    for c in range(NC):
-        rest_part(1, c, finish_second)
+    for c in range(NC - 1):
+        rest_part(1, c, None)
+    z_last[...] = z[NC - 1][...]
+    arrive(1, NC - 1)
 
     for j in range(NJ):
         @pl.when(has_source[j])
@@ -270,15 +291,32 @@
 
         @pl.when(has_dest[j])
         def _():
-            for tick in range(2):
-                for c in range(NC):
-                    block_copy(tick, j, c).wait_send()
+            sent = w_v.at[pl.ds(0, 2 * BLK)]
+            pltpu.make_async_copy(sent, sent, z_send.at[j]).wait()
 
     @pl.when(jnp.logical_not(last))
     def _():
-        init_copy().wait_send()
-        for n in range(NC):
-            hand_copy(n).wait_send()
+        pltpu.make_async_copy(w_v, w_v, x_send).wait()
+
+
+def finish_kernel(handed, acc, z_last, recv_last, a_hi, a_lo, w_hi, w_lo, handed_out, advanced_out, result, sem):
+    last = NC - 1
+    store = pltpu.make_async_copy(handed, handed_out, sem.at[NC])
+    store.start()
+    k = pl.ds(V, NJ * BLK)
+    feats = recv_last[...].reshape(V, WIDTHS[last])
+    parts = split(z_last[...] + adjacent(a_hi[:, k], a_lo[:, k], feats))
+
+    def store_part(n):
+        return pltpu.make_async_copy(result.at[:, :, cols(n)], advanced_out.at[:, :, cols(n)], sem.at[n])
+
+    for n in range(NC):
+        value = acc[:, cols(n)] + weighted(parts, w_hi[cols(last), cols(n)], w_lo[cols(last), cols(n)])
+        result[:, :, cols(n)] = jnp.maximum(value, 0.0).reshape(NB, BLK, WIDTHS[n])
+        store_part(n).start()
+    store.wait()
+    for n in range(NC):
+        store_part(n).wait()
 
 
 def blocks(x):
@@ -286,39 +324,42 @@
 
 
 def shards(n_seg, n_graph, state, initial, fresh, weights, wants, adj_slot, adj_count, adj_vals):
-    smem = pl.BlockSpec(memory_space=pltpu.SMEM)
     hbm = pl.BlockSpec(memory_space=pltpu.HBM)
     vmem = pl.BlockSpec(memory_space=pltpu.VMEM)
-    out = jax.ShapeDtypeStruct((NB, BLK, D), F32)
     dma = pltpu.SemaphoreType.DMA
-    handed, advanced = pl.pallas_call(
+    carried = (
+        pltpu.VMEM((NB, BLK, D), F32),
+        pltpu.VMEM((V, D), F32),
+        pltpu.VMEM((V, WIDTHS[-1]), F32),
+        pltpu.VMEM((NJ, BLK, WIDTHS[-1]), F32),
+        pltpu.VMEM((V, (NB + NJ) * BLK), BF16),
+        pltpu.VMEM((V, (NB + NJ) * BLK), BF16),
+        pltpu.VMEM((D, D), BF16),
+        pltpu.VMEM((D, D), BF16),
+    )
+    results = pl.pallas_call(
         functools.partial(kernel, n_seg, n_graph),
-        out_shape=(out, out),
+        out_shape=carried,
         in_specs=[hbm] * 8,
-        out_specs=(vmem, vmem),
+        out_specs=(vmem,) * len(carried),
         scratch_shapes=[
             pltpu.VMEM((NB, BLK, D), F32),
             pltpu.VMEM((NB, KMAX, BLK, BLK), F32),
             pltpu.VMEM((D, D), F32),
             pltpu.VMEM((NB, BLK, D), F32),
             pltpu.VMEM((NB, BLK, D), F32),
-            pltpu.VMEM((V, (NB + NJ) * BLK), BF16),
-            pltpu.VMEM((V, (NB + NJ) * BLK), BF16),
-            pltpu.VMEM((D, D), BF16),
-            pltpu.VMEM((D, D), BF16),
             pltpu.SMEM((NJ, NJ), jnp.int32),
             pltpu.SMEM((NB, KMAX), jnp.int32),
             pltpu.SMEM((NB,), jnp.int32),
         ]
         + [pltpu.VMEM((NB, BLK, w), F32) for _ in range(5) for w in WIDTHS]
-        + [pltpu.VMEM((V, w), F32) for _ in range(2) for w in WIDTHS]
+        + [pltpu.VMEM((V, w), F32) for w in WIDTHS]
         + [
-            dma((6,)), dma((NJ,)), dma((NJ,)), dma((2, NJ, NC)), dma((2, NJ, NC)),
-            dma((NC,)), dma((NC,)), dma, dma,
+            dma((6,)), dma((NJ,)), dma((NJ,)), dma((NJ,)), dma((2, NC)), dma, dma((NC,)), dma,
             pltpu.SemaphoreType.REGULAR,
         ],
         compiler_params=pltpu.CompilerParams(
-            collective_id=0, has_side_effects=True, vmem_limit_bytes=48 * 1024 * 1024
+            collective_id=0, has_side_effects=True, vmem_limit_bytes=40 * 1024 * 1024
         ),
     )(
         *(
@@ -329,6 +370,15 @@
             )
         )
     )
+    out = pltpu.HBM((NB, BLK, D), F32)
+    handed, advanced = pl.pallas_call(
+        finish_kernel,
+        out_shape=(out, out),
+        in_specs=[vmem] * len(carried),
+        out_specs=(hbm, hbm),
+        scratch_shapes=[pltpu.VMEM((NB, BLK, D), F32), dma((NC + 1,))],
+        compiler_params=pltpu.CompilerParams(vmem_limit_bytes=20 * 1024 * 1024),
+    )(*results)
     return handed.reshape(1, V, D), advanced.reshape(1, V, D)
 
 

time: 85.8 us -> 82.5 us (0.962)
  local copies, waits for them, and re-layouts: 2.64 us -> 0 us
    unnamed x2 -> x0, local copies, waits for them, and re-layouts: 2.64 us -> none
    pallas_call x1 -> x2, Pallas kernels: 82.1 us -> 81.6 us  [the longest x1 79.4 us: shards(): pl.pallas_call(functools.partial(kernel, n_seg, n_graph), out_shape=carri...]
where the time goes in v3:
time: 82.5 us; the launch traced here: 82.4 us
  Pallas kernels  81.6 us (99%)
    pallas_call x1, Pallas kernels, shards(): pl.pallas_call(functools.partial(kernel, n_seg, n_graph), out_shape=carri...  79.4 us
    pallas_call x1, Pallas kernels, shards(): pl.pallas_call(finish_kernel, out_shape=(out, out), in_specs=[vmem] * len...  2.14 us

profile of v3, /device:TPU:25, one launch (start us, length us, event | category | flops | bytes accessed | tf_op | source)
XLA Modules:
  0.0 82.4 jit_solution(10099953394729529260)
XLA Ops:
  0.6 79.4 %shard_map.95 = (f32[4,128,1024]{2,1,0:T(8,128)S(1)}, f32[512,1024]{1,0:T(8,128)S(1)}, f32[512,128]{1,0:T(8,128)S(1)}, f32[4,128,128]{2,1,0:T(8,128)S(1)}, bf16[...) custom-call(s32[4,4]{1,0:T(4,128)} %slot_hbm.1, ...), custom_call_target="tpu_custom_call" | custom-call | tf_op jit(solution)/shard_map/pallas_call | solution.py:340
  80.1 2.1 %shard_map.96 = (f32[4,128,1024]{2,1,0:T(8,128)}, f32[4,128,1024]{2,1,0:T(8,128)}) custom-call(f32[4,128,1024]{2,1,0:T(8,128)S(1)} %get-tuple-element.12.handed, f32[512,1024]{1,0:T(8,128)S(1)} %get-tuple-element.13.acc, f32[512,128]{1,0:T(8,128)S(1)} %get-tuple-element.14.z_last, f32[4,128,128]{2,1,0:T(8,128)S(1)} %get-tuple-element.15.recv_last, ...), custom_call_target="tpu_custom_call" | custom-call | tf_op jit(solution)/shard_map/pallas_call | solution.py:374

commit v4 on v3

--- a/solution.py
+++ b/solution.py
@@ -58,7 +58,7 @@
     n_seg, n_graph,
     slot_hbm, count_hbm, state, initial, fresh, weights, vals, wants_hbm,
     handed, acc, z_last, recv_last, a_hi, a_lo, w_hi, w_lo,
-    state_v, vals_v, w_v, init_v, init_in, wants_in, slot, count, *rest,
+    state_v, vals_v, w_v, init_v, init_in, wants_in, slot, count, wants, *rest,
 ):
     h_in, stage1, stage2, recv1, recv2, z = (rest[i * NC : (i + 1) * NC] for i in range(6))
     recv2 = recv2[: NC - 1] + (recv_last,)
@@ -77,9 +77,10 @@
     loads = [
         pltpu.make_async_copy(src, dst, load_sem.at[i])
         for i, (src, dst) in enumerate(
-            ((state, state_v), (vals, vals_v), (weights, w_v), (initial, init_v), (slot_hbm, slot), (count_hbm, count))
+            ((state, state_v), (vals, vals_v), (weights, w_v), (initial, init_v), (slot_hbm, slot), (count_hbm, count), (wants_hbm, wants))
         )
     ]
+    loads[6].start()
     loads[0].start()
 
     barrier = pltpu.get_barrier_semaphore()
@@ -103,7 +104,7 @@
 
     def want_copy(j):
         return pltpu.make_async_remote_copy(
-            src_ref=wants_hbm, dst_ref=wants_in.at[j], send_sem=want_send.at[j], recv_sem=want_recv.at[j],
+            src_ref=wants, dst_ref=wants_in.at[j], send_sem=want_send.at[j], recv_sem=want_recv.at[j],
             device_id={"graph": sources[j]}, device_id_type=MESH,
         )
 
@@ -113,12 +114,13 @@
             device_id={"segment": sec + 1}, device_id_type=MESH,
         )
 
+    loads[6].wait()
     for j in ORDER:
         @pl.when(has_source[j])
         def _():
             want_copy(j).start()
 
-    for load in loads[1:]:
+    for load in loads[1:6]:
         load.start()
 
     @pl.when(jnp.logical_not(last))
@@ -351,11 +353,12 @@
             pltpu.SMEM((NJ, NJ), jnp.int32),
             pltpu.SMEM((NB, KMAX), jnp.int32),
             pltpu.SMEM((NB,), jnp.int32),
+            pltpu.SMEM((NJ,), jnp.int32),
         ]
         + [pltpu.VMEM((NB, BLK, w), F32) for _ in range(5) for w in WIDTHS]
         + [pltpu.VMEM((V, w), F32) for w in WIDTHS]
         + [
-            dma((6,)), dma((NJ,)), dma((NJ,)), dma((NJ,)), dma((2, NC)), dma, dma((NC,)), dma,
+            dma((7,)), dma((NJ,)), dma((NJ,)), dma((NJ,)), dma((2, NC)), dma, dma((NC,)), dma,
             pltpu.SemaphoreType.REGULAR,
         ],
         compiler_params=pltpu.CompilerParams(

time: 82.5 us -> 82.2 us (level)
  no operation moved by 1% of the time
where the time goes in v4:
time: 82.2 us; the launch traced here: 82 us
  Pallas kernels  81.2 us (99%)
    pallas_call x1, Pallas kernels, shards(): pl.pallas_call(functools.partial(kernel, n_seg, n_graph), out_shape=carri...  79.1 us
    pallas_call x1, Pallas kernels, shards(): pl.pallas_call(finish_kernel, out_shape=(out, out), in_specs=[vmem] * len...  2.14 us

profile of v4, /device:TPU:25, one launch (start us, length us, event | category | flops | bytes accessed | tf_op | source)
XLA Modules:
  0.0 82.0 jit_solution(4271956820292383325)
XLA Ops:
  0.6 79.1 %shard_map.95 = (f32[4,128,1024]{2,1,0:T(8,128)S(1)}, f32[512,1024]{1,0:T(8,128)S(1)}, f32[512,128]{1,0:T(8,128)S(1)}, f32[4,128,128]{2,1,0:T(8,128)S(1)}, bf16[...) custom-call(s32[4,4]{1,0:T(4,128)} %slot_hbm.1, ...), custom_call_target="tpu_custom_call" | custom-call | tf_op jit(solution)/shard_map/pallas_call | solution.py:342
  79.7 2.1 %shard_map.96 = (f32[4,128,1024]{2,1,0:T(8,128)}, f32[4,128,1024]{2,1,0:T(8,128)}) custom-call(f32[4,128,1024]{2,1,0:T(8,128)S(1)} %get-tuple-element.12.handed, f32[512,1024]{1,0:T(8,128)S(1)} %get-tuple-element.13.acc, f32[512,128]{1,0:T(8,128)S(1)} %get-tuple-element.14.z_last, f32[4,128,128]{2,1,0:T(8,128)S(1)} %get-tuple-element.15.recv_last, ...), custom_call_target="tpu_custom_call" | custom-call | tf_op jit(solution)/shard_map/pallas_call | solution.py:377

commit v5 on v4

--- a/solution.py
+++ b/solution.py
@@ -303,22 +303,23 @@
 
 def finish_kernel(handed, acc, z_last, recv_last, a_hi, a_lo, w_hi, w_lo, handed_out, advanced_out, result, sem):
     last = NC - 1
-    store = pltpu.make_async_copy(handed, handed_out, sem.at[NC])
+    store = pltpu.make_async_copy(handed, handed_out, sem.at[NB])
     store.start()
     k = pl.ds(V, NJ * BLK)
     feats = recv_last[...].reshape(V, WIDTHS[last])
     parts = split(z_last[...] + adjacent(a_hi[:, k], a_lo[:, k], feats))
 
-    def store_part(n):
-        return pltpu.make_async_copy(result.at[:, :, cols(n)], advanced_out.at[:, :, cols(n)], sem.at[n])
-
-    for n in range(NC):
-        value = acc[:, cols(n)] + weighted(parts, w_hi[cols(last), cols(n)], w_lo[cols(last), cols(n)])
-        result[:, :, cols(n)] = jnp.maximum(value, 0.0).reshape(NB, BLK, WIDTHS[n])
-        store_part(n).start()
+    def store_part(b):
+        return pltpu.make_async_copy(result.at[b], advanced_out.at[b], sem.at[b])
+
+    for b in range(NB):
+        rows = slice(b * BLK, (b + 1) * BLK)
+        value = acc[rows, :] + weighted([p[rows] for p in parts], w_hi[cols(last), :], w_lo[cols(last), :])
+        result[b] = jnp.maximum(value, 0.0)
+        store_part(b).start()
     store.wait()
-    for n in range(NC):
-        store_part(n).wait()
+    for b in range(NB):
+        store_part(b).wait()
 
 
 def blocks(x):
@@ -379,7 +380,7 @@
         out_shape=(out, out),
         in_specs=[vmem] * len(carried),
         out_specs=(hbm, hbm),
-        scratch_shapes=[pltpu.VMEM((NB, BLK, D), F32), dma((NC + 1,))],
+        scratch_shapes=[pltpu.VMEM((NB, BLK, D), F32), dma((NB + 1,))],
         compiler_params=pltpu.CompilerParams(vmem_limit_bytes=20 * 1024 * 1024),
     )(*results)
     return handed.reshape(1, V, D), advanced.reshape(1, V, D)

time: 82.2 us -> 82.1 us (level)
  no operation moved by 1% of the time
where the time goes in v5:
time: 82.1 us; the launch traced here: 82 us
  Pallas kernels  81.2 us (99%)
    pallas_call x1, Pallas kernels, shards(): pl.pallas_call(functools.partial(kernel, n_seg, n_graph), out_shape=carri...  79.1 us
    pallas_call x1, Pallas kernels, shards(): pl.pallas_call(finish_kernel, out_shape=(out, out), in_specs=[vmem] * len...  2.05 us

profile of v5, /device:TPU:25, one launch (start us, length us, event | category | flops | bytes accessed | tf_op | source)
XLA Modules:
  0.0 82.0 jit_solution(7250367334810244084)
XLA Ops:
  0.6 79.1 %shard_map.95 = (f32[4,128,1024]{2,1,0:T(8,128)S(1)}, f32[512,1024]{1,0:T(8,128)S(1)}, f32[512,128]{1,0:T(8,128)S(1)}, f32[4,128,128]{2,1,0:T(8,128)S(1)}, bf16[...) custom-call(s32[4,4]{1,0:T(4,128)} %slot_hbm.1, ...), custom_call_target="tpu_custom_call" | custom-call | tf_op jit(solution)/shard_map/pallas_call | solution.py:343
  79.7 2.0 %shard_map.96 = (f32[4,128,1024]{2,1,0:T(8,128)}, f32[4,128,1024]{2,1,0:T(8,128)}) custom-call(f32[4,128,1024]{2,1,0:T(8,128)S(1)} %get-tuple-element.12.handed, f32[512,1024]{1,0:T(8,128)S(1)} %get-tuple-element.13.acc, f32[512,128]{1,0:T(8,128)S(1)} %get-tuple-element.14.z_last, f32[4,128,128]{2,1,0:T(8,128)S(1)} %get-tuple-element.15.recv_last, ...), custom_call_target="tpu_custom_call" | custom-call | tf_op jit(solution)/shard_map/pallas_call | solution.py:378
